TPU v7x, 512 devices: a whole 4x4x16 slice. The times are simulated.
512 devices in a mesh: blk: 32 (over x, z_lo), rep: 16 (over z_hi, y, core).
Axes of the slice: x: 4, y: 4, z: 16 (z_hi: 2, z_lo: 8; z = z_hi * 8 + z_lo), core: 2. Of those that a mesh axis runs over, the one named last changes fastest.
Arguments:
- signals: bfloat16 [32768, 8192], P('rep', 'blk'), may hold values from -6 to 6
- omega: float32 [32, 5, 256, 256], P('blk', None, 'rep'), may hold values from -1.2 to 3, as said below
- pattern: int32 [32, 5], P('blk'), may hold values from 0 to 31, as said below
Outputs:
- omega_next: float32 [32, 5, 256, 256], P('blk', None, 'rep')
Inputs may be any that keep to these rules, and one draw needn't show every extreme that they name: pattern[i, 0] = i. For two distinct whole numbers A and B from 1 to 15, the same in every row, pattern[i, 1] to pattern[i, 4] are i + A, i - A, i + B and i - B modulo 32 in some order, the same order in every row. Omega is symmetric: omega[i, k] is the transpose of omega[pattern[i, k], k2] where pattern[pattern[i, k], k2] = i. The diagonal entries of omega[i, 0] lie between 1 and 3.
All inputs are finite; a program needn't handle non-finite values.
Results may differ from a plain program's by a relative error of at most 0.0033.
Values may be sent and summed in bfloat16 or wider, within the bound.
A program may use at most 128 MiB of HBM per device.

v0:
```python
import jax
import jax.numpy as jnp
from jax import lax
from jax.sharding import Mesh
from jax.sharding import PartitionSpec as P

STEP_SIZE = 0.5
PENALTY = 0.1
REP = ("zh", "y", "c")


def fine_mesh(mesh):
    return Mesh(mesh.devices.reshape(4, 8, 2, 4, 2), ("x", "zl", "zh", "y", "c"))


def per_device(signals, omega, pattern):
    x_size = lax.axis_size("x")
    zl_size = lax.axis_size("zl")
    team_count = x_size * zl_size
    replica_count = lax.axis_size(REP)
    team_index = lax.axis_index(("x", "zl"))
    replica_index = lax.axis_index(REP)
    slot_count, tile_rows, width = omega.shape[1:]
    time_length = signals.shape[0] * replica_count
    offsets = jnp.mod(pattern[0] - team_index, team_count)
    own = signals.reshape(zl_size, signals.shape[0] // zl_size, width)
    blocks = lax.all_to_all(own, "zl", 0, 0, tiled=True)
    blocks = lax.all_gather(blocks, "x", axis=0, tiled=True)
    panels = lax.all_gather(omega.astype(jnp.bfloat16), REP, axis=2, tiled=True)
    panels = lax.all_gather(panels, "zl", axis=0, tiled=True)
    rows = lax.axis_index("x") * zl_size + jnp.arange(zl_size, dtype=jnp.int32)
    columns = jnp.mod(rows[:, None] + offsets[None, :], team_count)
    gathered = blocks[columns]
    mixed = jnp.einsum(
        "jktc,jkdc->jtd", gathered, panels, preferred_element_type=jnp.float32
    ).astype(jnp.bfloat16)
    left = jnp.einsum("jtd,jktc->jkdc", mixed, gathered, preferred_element_type=jnp.float32)
    own_terms = lax.psum_scatter(left, REP, scatter_dimension=2, tiled=True)
    own_terms = lax.psum_scatter(own_terms, "zl", scatter_dimension=0, tiled=True)[0]
    flipped = lax.all_to_all(own_terms, REP, 2, 1, tiled=True)
    flipped = jnp.swapaxes(flipped, 1, 2)
    match = offsets[None, :] == jnp.mod(team_count - offsets, team_count)[:, None]
    mirror = jnp.argmax(match, axis=1)
    outgoing = flipped[mirror]
    for level in range(team_count.bit_length() - 1):
        step = 1 << level
        route = [((i + step) % team_count, i) for i in range(team_count)]
        shifted = lax.ppermute(outgoing, ("x", "zl"), route)
        chosen = jnp.mod(offsets // step, 2) == 1
        outgoing = jnp.where(chosen[:, None, None], shifted, outgoing)
    gradient = (own_terms + outgoing) / (2.0 * time_length)
    tiles = omega[0]
    column_ids = jnp.arange(width, dtype=jnp.int32)
    row_ids = replica_index * tile_rows + jnp.arange(tile_rows, dtype=jnp.int32)
    diagonal = column_ids[None, :] == row_ids[:, None]
    diagonal = diagonal[None] & (offsets == 0)[:, None, None]
    gradient = gradient - jnp.where(diagonal, 1.0 / jnp.where(diagonal, tiles, 1.0), 0.0)
    value = tiles - STEP_SIZE * gradient
    shrunk = jnp.sign(value) * jnp.maximum(jnp.abs(value) - STEP_SIZE * PENALTY, 0.0)
    return jnp.where(diagonal, value, shrunk)[None]


def solution(mesh):
    return jax.shard_map(
        per_device,
        mesh=fine_mesh(mesh),
        in_specs=(P(REP, ("x", "zl")), P(("x", "zl"), None, REP, None), P(("x", "zl"), None)),
        out_specs=P(("x", "zl"), None, REP, None),
        check_vma=False,
    )
```

profile of v0, /device:TPU:230, one launch (start us, length us, event | category | flops | bytes accessed | tf_op | source)
XLA Modules:
  0.0 669.5 jit_solution(8638916152552195182)
XLA Ops:
  6.5 0.0 all-gather.3.cloned.1.call-start
  6.5 55.6 %all_to_all.23 = bf16[8,256,256]{2,1,0:T(8,128)(2,1)} all-to-all(bf16[8,256,256]{2,1,0:T(8,128)(2,1)} %bitcast.50), channel_id=1, replica_groups=mesh['x'=4,'zl'=8,'zh'=2,'y'=4,'c'=2] {'zl'}, dimensions={0} | all-to-all | bytes 2097152 | tf_op jit(solution)/shard_map/all_to_all | solution.py:27
  62.1 0.0 all-gather.3.cloned.1.call-update
  62.1 0.0 all-gather.5.cloned.1.call-start
  62.2 0.9 convert_element_type.6
  63.1 45.3 %all_gather.10 = bf16[1,5,256,256]{3,2,1,0:T(8,128)(2,1)} all-gather(bf16[1,5,16,256]{3,2,1,0:T(8,128)(2,1)S(1)} %convert_element_type.6), channel_id=1, replica_groups=mesh['x'=4,'zl'=8,'zh'=2,'y'=4,'c'=2] {'zh','y','c'}, dimensions={2}, use_global_device_ids=true | all-gather | bytes 696320 | tf_op jit(solution)/shard_map/all_gather | solution.py:29
  108.4 0.0 all-gather.5.cloned.1.call-update
  108.4 0.0 reduce-scatter.3.cloned.1.call-start
  108.5 0.7 fusion.7
  109.2 0.1 compare_select_fusion
  109.2 0.1 reshape.294
  109.3 10.0 %all-gather.3.cloned.1.call-done = bf16[32,256,256]{2,1,0:T(8,128)(2,1)} async-done(((bf16[8,256,256]{2,1,0:T(8,128)(2,1)}), bf16[32,256,256]{2,1,0:T(8,128)(2,1)}) %all-gather.3.cloned.1.call-update) | async-done | bytes 4194320 | tf_op jit(solution)/shard_map/all_gather | solution.py:28
  119.3 6.7 %gather_fusion = bf16[40,256,256]{2,1,0:T(8,128)(2,1)} fusion(bf16[32,256,256]{2,1,0:T(8,128)(2,1)} %all-gather.3.cloned.1.call-done, s32[1024]{0:T(1024)S(1)} %pad_clamp_fusion.1), kind=kCustom, calls=%fused_computation | custom fusion | bytes 10485920 | tf_op jit(solution)/shard_map/gather | solution.py:33
  126.0 114.0 %all-gather.5.cloned.1.call-done = bf16[8,5,256,256]{3,2,1,0:T(8,128)(2,1)} async-done(((bf16[1,5,256,256]{3,2,1,0:T(8,128)(2,1)}), bf16[8,5,256,256]{3,2,1,0:T(8,128)(2,1)}) %all-gather.5.cloned.1.call-update) | async-done | bytes 5242896 | tf_op jit(solution)/shard_map/all_gather | solution.py:30
  240.0 12.5 %convolution_bitcast_fusion = f32[8,5,256,256]{2,3,1,0:T(8,128)} fusion(bf16[8,5,256,256]{3,2,1,0:T(8,128)(2,1)} %bitcast.46, bf16[8,5,256,256]{3,2,1,0:T(8,128)(2,1)} %all-gather.5.cloned.1.call-done), kind=kOutput, calls=%fused_computation.2 | convolution fusion | flops 2684878848 | bytes 20971520 | tf_op jit(solution)/shard_map/jtd,jktc->jkdc/dot_general | solution.py:37
  252.5 11.6 %copy.24 = f32[8,5,256,256]{3,0,1,2:T(8,128)} copy(f32[8,5,256,256]{2,3,1,0:T(8,128)} %convolution_bitcast_fusion) | data formatting | bytes 20971520 | tf_op jit(solution)/shard_map/jtd,jktc->jkdc/transpose | solution.py:37
  264.1 0.0 copy-start.2
  264.1 0.0 reduce-scatter.3.cloned.1.call-update
  264.2 0.0 copy-start.1
  264.2 0.0 reduce-scatter.5.cloned.1.call-start
  264.2 245.1 %reduce-scatter.3.cloned.1.call-done = f32[8,5,16,256]{3,0,1,2:T(8,128)} async-done(((f32[8,5,256,256]{3,0,1,2:T(8,128)}), f32[8,5,16,256]{3,0,1,2:T(8,128)}) %reduce-scatter.3.cloned.1.call-update) | async-done | bytes 655376 | tf_op jit(solution)/shard_map/reduce_scatter | solution.py:38
  509.3 2.1 copy.25
  511.5 0.0 reduce-scatter.5.cloned.1.call-update
  511.5 0.0 copy-done.2
  511.5 0.7 iota_reduce_fusion
  512.2 58.2 %reduce-scatter.5.cloned.1.call-done = f32[1,5,16,256]{3,2,1,0:T(8,128)} async-done(((f32[8,5,16,256]{3,2,1,0:T(8,128)}), f32[1,5,16,256]{3,2,1,0:T(8,128)}) %reduce-scatter.5.cloned.1.call-update) | async-done | bytes 81936 | tf_op jit(solution)/shard_map/reduce_scatter | solution.py:39
  570.4 0.0 copy-start
  570.4 1.4 copy.26
  571.8 1.0 reshape.312
  572.8 14.2 %all-to-all-start.1 = ((f32[16,1,1280]{2,1,0:T(1,128)}), f32[16,1,1280]{2,1,0:T(1,128)S(1)}, u32[]{:S(2)}, u32[]{:S(2)}) async-start(f32[16,1,1280]{2,1,0:T(1,128)} %reshape.312), calls=%async_computation.3 | async-start | bytes 163840 | tf_op jit(solution)/shard_map/all_to_all | solution.py:40
  587.0 15.0 %all-to-all-done.1 = f32[16,1,1280]{2,1,0:T(1,128)S(1)} async-done(((f32[16,1,1280]{2,1,0:T(1,128)}), f32[16,1,1280]{2,1,0:T(1,128)S(1)}, u32[]{:S(2)}, u32[]{:S(2)}) %all-to-all-start.1) | async-done | bytes 81952 | tf_op jit(solution)/shard_map/all_to_all | solution.py:40
  602.0 0.5 broadcast.611
  602.5 0.8 reduce.19
  603.4 0.3 reshape.313
  603.7 0.4 copy.32
  604.1 0.3 all_to_all.20
  604.4 0.6 gather_fusion.1
  604.9 1.9 collective-permute-start
  606.9 13.1 %collective-permute-done = f32[5,16,256]{2,1,0:T(8,128)S(1)} collective-permute-done((f32[5,16,256]{2,1,0:T(8,128)S(1)}, f32[5,16,256]{2,1,0:T(8,128)S(1)}, u32[]{:S(2)}, u32[]{:S(2)}) %collective-permute-start) | collective-permute-done | bytes 81952 | tf_op jit(solution)/shard_map/ppermute | solution.py:48
  620.0 0.1 broadcast_select_fusion
  620.1 1.9 collective-permute-start.1
  622.0 12.3 %collective-permute-done.1 = f32[5,16,256]{2,1,0:T(8,128)S(1)} collective-permute-done((f32[5,16,256]{2,1,0:T(8,128)S(1)}, f32[5,16,256]{2,1,0:T(8,128)S(1)}, u32[]{:S(2)}, u32[]{:S(2)}) %collective-permute-start.1) | collective-permute-done | bytes 81952 | tf_op jit(solution)/shard_map/ppermute | solution.py:48
  634.2 0.1 broadcast_select_fusion.1
  634.3 1.9 collective-permute-start.2
  636.2 10.4 %collective-permute-done.2 = f32[5,16,256]{2,1,0:T(8,128)S(1)} collective-permute-done((f32[5,16,256]{2,1,0:T(8,128)S(1)}, f32[5,16,256]{2,1,0:T(8,128)S(1)}, u32[]{:S(2)}, u32[]{:S(2)}) %collective-permute-start.2) | collective-permute-done | bytes 81952 | tf_op jit(solution)/shard_map/ppermute | solution.py:48
  646.7 0.1 broadcast_select_fusion.2
  646.7 1.9 collective-permute-start.3
  648.7 5.6 collective-permute-done.3
  654.3 0.1 broadcast_select_fusion.3
  654.3 1.9 collective-permute-start.4
  656.3 0.1 iota_compare_fusion
  656.3 5.8 collective-permute-done.4
  662.2 0.0 copy-done.1
  662.2 0.0 copy-done
  662.2 0.8 fusion.5
  (8 shorter events, 0.1 us)
Async XLA Ops:
  6.5 112.7 %all-gather.3.cloned.1.call-start = ((), (), s32[]{:S(2)}) async-start(), calls=%async_computation.4 | async-start | bytes 5242880 | tf_op jit(solution)/shard_map/all_gather | solution.py:28
  62.1 177.9 %all-gather.5.cloned.1.call-start = ((), (), s32[]{:S(2)}) async-start(), calls=%async_computation.5 | async-start | bytes 5898240 | tf_op jit(solution)/shard_map/all_gather | solution.py:30
  108.4 400.9 %reduce-scatter.3.cloned.1.call-start = ((), (), s32[]{:S(2)}) async-start(), calls=%async_computation.6 | async-start | bytes 11141120 | tf_op jit(solution)/shard_map/reduce_scatter | solution.py:38
  264.1 247.4 %copy-start.2 = (s32[1,5]{1,0:T(1,128)S(1)}, s32[1,5]{1,0:T(1,128)}, u32[]{:S(2)}) copy-start(s32[1,5]{1,0:T(1,128)} %param.5) | copy-start | bytes 64
  264.2 398.0 %copy-start.1 = (f32[1,5,16,256]{3,2,1,0:T(8,128)S(1)}, f32[1,5,16,256]{3,2,1,0:T(8,128)}, u32[]{:S(2)}) copy-start(f32[1,5,16,256]{3,2,1,0:T(8,128)} %param.4) | copy-start | bytes 245764
  264.2 306.2 %reduce-scatter.5.cloned.1.call-start = ((), (), s32[]{:S(2)}) async-start(), calls=%async_computation.7 | async-start | bytes 737280 | tf_op jit(solution)/shard_map/reduce_scatter | solution.py:39
  570.4 91.8 %copy-start = (f32[1,5,16,256]{3,2,1,0:T(8,128)S(1)}, f32[1,5,16,256]{3,2,1,0:T(8,128)}, u32[]{:S(2)}) copy-start(f32[1,5,16,256]{3,2,1,0:T(8,128)} %reduce-scatter.5.cloned.1.call-done) | copy-start | bytes 245764
  572.8 29.2 %all-to-all-start.1 = ((f32[16,1,1280]{2,1,0:T(1,128)}), f32[16,1,1280]{2,1,0:T(1,128)S(1)}, u32[]{:S(2)}, u32[]{:S(2)}) async-start(f32[16,1,1280]{2,1,0:T(1,128)} %reshape.312), calls=%async_computation.3 | async-start | bytes 163840 | tf_op jit(solution)/shard_map/all_to_all | solution.py:40
  604.9 15.0 %collective-permute-start = (f32[5,16,256]{2,1,0:T(8,128)S(1)}, f32[5,16,256]{2,1,0:T(8,128)S(1)}, u32[]{:S(2)}, u32[]{:S(2)}) collective-permute-start(f32[5,16,256]{2,1,0:T(8,128)S(1)} %gather_fusion.1), channel_id=1, source_target_pairs={{16,0},{32,16},{48,32},{64,48},{80,64},{96,80},{112,96},{128,112},... | collective-permute-start | bytes 245768 | tf_op jit(solution)/shard_map/ppermute | solution.py:48
  620.1 14.2 %collective-permute-start.1 = (f32[5,16,256]{2,1,0:T(8,128)S(1)}, f32[5,16,256]{2,1,0:T(8,128)S(1)}, u32[]{:S(2)}, u32[]{:S(2)}) collective-permute-start(f32[5,16,256]{2,1,0:T(8,128)S(1)} %broadcast_select_fusion), channel_id=1, source_target_pairs={{32,0},{48,16},{64,32},{80,48},{96,64},{112,80},{128,96},{144,112}... | collective-permute-start | bytes 245768 | tf_op jit(solution)/shard_map/ppermute | solution.py:48
  634.3 12.3 %collective-permute-start.2 = (f32[5,16,256]{2,1,0:T(8,128)S(1)}, f32[5,16,256]{2,1,0:T(8,128)S(1)}, u32[]{:S(2)}, u32[]{:S(2)}) collective-permute-start(f32[5,16,256]{2,1,0:T(8,128)S(1)} %broadcast_select_fusion.1), channel_id=1, source_target_pairs={{64,0},{80,16},{96,32},{112,48},{128,64},{144,80},{160,96},{176,11... | collective-permute-start | bytes 245768 | tf_op jit(solution)/shard_map/ppermute | solution.py:48
  646.7 7.5 %collective-permute-start.3 = (f32[5,16,256]{2,1,0:T(8,128)S(1)}, f32[5,16,256]{2,1,0:T(8,128)S(1)}, u32[]{:S(2)}, u32[]{:S(2)}) collective-permute-start(f32[5,16,256]{2,1,0:T(8,128)S(1)} %broadcast_select_fusion.2), channel_id=1, source_target_pairs={{128,0},{144,16},{160,32},{176,48},{192,64},{208,80},{224,96},{240... | collective-permute-start | bytes 245768 | tf_op jit(solution)/shard_map/ppermute | solution.py:48
  654.3 7.8 %collective-permute-start.4 = (f32[5,16,256]{2,1,0:T(8,128)S(1)}, f32[5,16,256]{2,1,0:T(8,128)S(1)}, u32[]{:S(2)}, u32[]{:S(2)}) collective-permute-start(f32[5,16,256]{2,1,0:T(8,128)S(1)} %broadcast_select_fusion.3), channel_id=1, source_target_pairs={{256,0},{272,16},{288,32},{304,48},{320,64},{336,80},{352,96},{368... | collective-permute-start | bytes 245768 | tf_op jit(solution)/shard_map/ppermute | solution.py:48
Sparse Core Ops, SparseCore 0:
  62.2 56.9 all-gather.2
  121.4 118.6 all-gather.4
  264.3 245.0 reduce-scatter.2
  512.3 58.1 reduce-scatter.4
where the time goes:
time: 670 us; the launch traced here: 669 us
  waiting for transfers between devices  490 us (73%)
  blocking collectives  101 us (15%)
  local copies, waits for them, and re-layouts  25 us (4%)
  starting transfers between devices  23.9 us (4%)
  between operations  13.3 us (2%)
  matrix products  12.5 us (2%)
    reduce_scatter x1, waiting for transfers between devices, per_device(): own_terms = lax.psum_scatter(left, REP, scatter_dimension=2, tiled=True)  245 us
    all_gather x1, waiting for transfers between devices, per_device(): panels = lax.all_gather(panels, 'zl', axis=0, tiled=True)  114 us
    reduce_scatter x1, waiting for transfers between devices, per_device(): lax.psum_scatter(own_terms, 'zl', scatter_dimension=0, tiled=True)[0]  58.2 us
    all_to_all x1, blocking collectives, per_device(): blocks = lax.all_to_all(own, 'zl', 0, 0, tiled=True)  55.6 us
    ppermute x5, waiting for transfers between devices, per_device(): shifted = lax.ppermute(outgoing, ('x', 'zl'), route)  47.2 us
    all_gather x1, blocking collectives, per_device(): panels = lax.all_gather(omega.astype(jnp.bfloat16), REP, axis=2, tiled=True)  45.3 us
    all_to_all x1, waiting for transfers between devices, per_device(): flipped = lax.all_to_all(own_terms, REP, 2, 1, tiled=True)  15 us
    all_to_all x1, starting transfers between devices, per_device(): flipped = lax.all_to_all(own_terms, REP, 2, 1, tiled=True)  14.2 us
  transfers between devices with their start and end apart: 10, of which 10 were waited for; matrix products, arithmetic and copies ran while one was open for 1% of the time, Pallas kernels for 0%

commit v1 on v0

--- a/solution.py
+++ b/solution.py
@@ -3,6 +3,7 @@
 from jax import lax
 from jax.sharding import Mesh
 from jax.sharding import PartitionSpec as P
+from jax.lax import all_to_all, axis_size
 
 STEP_SIZE = 0.5
 PENALTY = 0.1
@@ -37,7 +38,9 @@
     left = jnp.einsum("jtd,jktc->jkdc", mixed, gathered, preferred_element_type=jnp.float32)
     own_terms = lax.psum_scatter(left, REP, scatter_dimension=2, tiled=True)
     own_terms = lax.psum_scatter(own_terms, "zl", scatter_dimension=0, tiled=True)[0]
-    flipped = lax.all_to_all(own_terms, REP, 2, 1, tiled=True)
+    flipped = jnp.concatenate(
+        all_to_all(jnp.stack(jnp.split(own_terms, axis_size(REP), axis=2)), REP, 0, 0), axis=1
+    )
     flipped = jnp.swapaxes(flipped, 1, 2)
     match = offsets[None, :] == jnp.mod(team_count - offsets, team_count)[:, None]
     mirror = jnp.argmax(match, axis=1)

time: 670 us -> 683 us (1.019)
  local copies, waits for them, and re-layouts: 25 us -> 37 us
    unnamed x8 -> x23, local copies, waits for them, and re-layouts: 1.32 us -> 13.9 us
where the time goes in v1:
time: 683 us; the launch traced here: 681 us
  waiting for transfers between devices  489 us (72%)
  blocking collectives  101 us (15%)
  local copies, waits for them, and re-layouts  37 us (5%)
  starting transfers between devices  23.9 us (3%)
  between operations  13.3 us (2%)
  matrix products  12.5 us (2%)
    reduce_scatter x1, waiting for transfers between devices, per_device(): own_terms = lax.psum_scatter(left, REP, scatter_dimension=2, tiled=True)  245 us
    all_gather x1, waiting for transfers between devices, per_device(): panels = lax.all_gather(panels, 'zl', axis=0, tiled=True)  114 us
    reduce_scatter x1, waiting for transfers between devices, per_device(): lax.psum_scatter(own_terms, 'zl', scatter_dimension=0, tiled=True)[0]  58.2 us
    all_to_all x1, blocking collectives, per_device(): blocks = lax.all_to_all(own, 'zl', 0, 0, tiled=True)  55.6 us
    ppermute x5, waiting for transfers between devices, per_device(): shifted = lax.ppermute(outgoing, ('x', 'zl'), route)  47.2 us
    all_gather x1, blocking collectives, per_device(): panels = lax.all_gather(omega.astype(jnp.bfloat16), REP, axis=2, tiled=True)  45.3 us
    all_to_all x1, waiting for transfers between devices, per_device(): all_to_all(jnp.stack(jnp.split(own_terms, axis_size(REP), axis=2)), REP,...  15 us
    all_to_all x1, starting transfers between devices, per_device(): all_to_all(jnp.stack(jnp.split(own_terms, axis_size(REP), axis=2)), REP,...  14.2 us
  transfers between devices with their start and end apart: 10, of which 10 were waited for; matrix products, arithmetic and copies ran while one was open for 1% of the time, Pallas kernels for 0%

profile of v1, /device:TPU:230, one launch (start us, length us, event | category | flops | bytes accessed | tf_op | source)
XLA Modules:
  0.0 681.4 jit_solution(17400444968461769958)
XLA Ops:
  6.5 55.6 %all_to_all.10 = bf16[8,256,256]{2,1,0:T(8,128)(2,1)} all-to-all(bf16[8,256,256]{2,1,0:T(8,128)(2,1)} %bitcast.123), channel_id=1, replica_groups=mesh['x'=4,'zl'=8,'zh'=2,'y'=4,'c'=2] {'zl'}, dimensions={0} | all-to-all | bytes 2097152 | tf_op jit(solution)/shard_map/all_to_all | solution.py:28
  62.1 0.0 all-gather.3.cloned.1.call-update
  62.1 0.0 all-gather.5.cloned.1.call-start
  62.2 0.9 convert_element_type.6
  63.1 45.3 %all_gather.10 = bf16[1,5,256,256]{3,2,1,0:T(8,128)(2,1)} all-gather(bf16[1,5,16,256]{3,2,1,0:T(8,128)(2,1)S(1)} %convert_element_type.6), channel_id=1, replica_groups=mesh['x'=4,'zl'=8,'zh'=2,'y'=4,'c'=2] {'zh','y','c'}, dimensions={2}, use_global_device_ids=true | all-gather | bytes 696320 | tf_op jit(solution)/shard_map/all_gather | solution.py:30
  108.4 0.0 all-gather.5.cloned.1.call-update
  108.4 0.0 reduce-scatter.3.cloned.1.call-start
  108.5 0.7 fusion.23
  109.2 0.1 compare_select_fusion
  109.2 0.1 reshape.302
  109.3 10.0 %all-gather.3.cloned.1.call-done = bf16[32,256,256]{2,1,0:T(8,128)(2,1)} async-done(((bf16[8,256,256]{2,1,0:T(8,128)(2,1)}), bf16[32,256,256]{2,1,0:T(8,128)(2,1)}) %all-gather.3.cloned.1.call-update) | async-done | bytes 4194320 | tf_op jit(solution)/shard_map/all_gather | solution.py:29
  119.3 6.7 gather_fusion
  126.0 114.0 %all-gather.5.cloned.1.call-done = bf16[8,5,256,256]{3,2,1,0:T(8,128)(2,1)} async-done(((bf16[1,5,256,256]{3,2,1,0:T(8,128)(2,1)}), bf16[8,5,256,256]{3,2,1,0:T(8,128)(2,1)}) %all-gather.5.cloned.1.call-update) | async-done | bytes 5242896 | tf_op jit(solution)/shard_map/all_gather | solution.py:31
  240.0 12.5 %convolution_bitcast_fusion = f32[8,5,256,256]{2,3,1,0:T(8,128)} fusion(bf16[8,5,256,256]{3,2,1,0:T(8,128)(2,1)} %bitcast.105, bf16[8,5,256,256]{3,2,1,0:T(8,128)(2,1)} %all-gather.5.cloned.1.call-done), kind=kOutput, calls=%fused_computation.2 | convolution fusion | flops 2684878848 | bytes 20971520 | tf_op jit(solution)/shard_map/jtd,jktc->jkdc/dot_general | solution.py:38
  252.5 11.6 %copy.23 = f32[8,5,256,256]{3,0,1,2:T(8,128)} copy(f32[8,5,256,256]{2,3,1,0:T(8,128)} %convolution_bitcast_fusion) | data formatting | bytes 20971520 | tf_op jit(solution)/shard_map/jtd,jktc->jkdc/transpose | solution.py:38
  264.1 0.0 reduce-scatter.3.cloned.1.call-update
  264.2 0.0 copy-start.1
  264.2 0.0 reduce-scatter.5.cloned.1.call-start
  264.2 245.1 %reduce-scatter.3.cloned.1.call-done = f32[8,5,16,256]{3,0,1,2:T(8,128)} async-done(((f32[8,5,256,256]{3,0,1,2:T(8,128)}), f32[8,5,16,256]{3,0,1,2:T(8,128)}) %reduce-scatter.3.cloned.1.call-update) | async-done | bytes 655376 | tf_op jit(solution)/shard_map/reduce_scatter | solution.py:39
  509.3 2.1 copy.24
  511.5 0.0 reduce-scatter.5.cloned.1.call-update
  511.5 0.7 iota_reduce_fusion
  512.2 58.2 %reduce-scatter.5.cloned.1.call-done = f32[1,5,16,256]{3,2,1,0:T(8,128)} async-done(((f32[8,5,16,256]{3,2,1,0:T(8,128)}), f32[1,5,16,256]{3,2,1,0:T(8,128)}) %reduce-scatter.5.cloned.1.call-update) | async-done | bytes 81936 | tf_op jit(solution)/shard_map/reduce_scatter | solution.py:40
  570.4 0.9 fusion.21
  571.3 0.9 fusion.20
  572.1 0.9 fusion.19
  573.0 0.9 fusion.18
  573.8 0.9 fusion.17
  574.7 0.9 fusion.16
  575.6 0.9 fusion.15
  576.4 0.9 fusion.14
  577.3 0.8 fusion.13
  578.1 0.9 fusion.12
  578.9 0.9 fusion.11
  579.8 0.9 fusion.10
  580.6 0.9 fusion.9
  581.5 0.9 fusion.8
  582.3 0.9 fusion.7
  583.2 0.9 fusion.6
  584.1 0.9 reshape.320
  585.0 14.2 %all-to-all-start.1 = ((f32[16,1,1280]{2,1,0:T(1,128)}), f32[16,1,1280]{2,1,0:T(1,128)S(1)}, u32[]{:S(2)}, u32[]{:S(2)}) async-start(f32[16,1,1280]{2,1,0:T(1,128)} %reshape.320), calls=%async_computation.3 | async-start | bytes 163840 | tf_op jit(solution)/shard_map/all_to_all | solution.py:42
  599.2 15.0 %all-to-all-done.1 = f32[16,1,1280]{2,1,0:T(1,128)S(1)} async-done(((f32[16,1,1280]{2,1,0:T(1,128)}), f32[16,1,1280]{2,1,0:T(1,128)S(1)}, u32[]{:S(2)}, u32[]{:S(2)}) %all-to-all-start.1) | async-done | bytes 81952 | tf_op jit(solution)/shard_map/all_to_all | solution.py:42
  614.1 0.5 broadcast.611
  614.6 0.8 reduce.19
  615.5 0.2 reshape.321
  615.7 0.3 copy.25
  616.1 0.3 reshape.299
  616.4 0.6 gather_fusion.1
  616.9 1.9 collective-permute-start
  618.9 13.1 %collective-permute-done = f32[5,16,256]{2,1,0:T(8,128)S(1)} collective-permute-done((f32[5,16,256]{2,1,0:T(8,128)S(1)}, f32[5,16,256]{2,1,0:T(8,128)S(1)}, u32[]{:S(2)}, u32[]{:S(2)}) %collective-permute-start) | collective-permute-done | bytes 81952 | tf_op jit(solution)/shard_map/ppermute | solution.py:51
  632.0 0.1 broadcast_select_fusion
  632.0 1.9 collective-permute-start.1
  634.0 12.2 %collective-permute-done.1 = f32[5,16,256]{2,1,0:T(8,128)S(1)} collective-permute-done((f32[5,16,256]{2,1,0:T(8,128)S(1)}, f32[5,16,256]{2,1,0:T(8,128)S(1)}, u32[]{:S(2)}, u32[]{:S(2)}) %collective-permute-start.1) | collective-permute-done | bytes 81952 | tf_op jit(solution)/shard_map/ppermute | solution.py:51
  646.2 0.1 broadcast_select_fusion.1
  646.3 1.9 collective-permute-start.2
  648.2 10.4 %collective-permute-done.2 = f32[5,16,256]{2,1,0:T(8,128)S(1)} collective-permute-done((f32[5,16,256]{2,1,0:T(8,128)S(1)}, f32[5,16,256]{2,1,0:T(8,128)S(1)}, u32[]{:S(2)}, u32[]{:S(2)}) %collective-permute-start.2) | collective-permute-done | bytes 81952 | tf_op jit(solution)/shard_map/ppermute | solution.py:51
  658.6 0.1 broadcast_select_fusion.2
  658.7 1.9 collective-permute-start.3
  660.6 5.6 collective-permute-done.3
  666.2 0.1 broadcast_select_fusion.3
  666.3 1.9 collective-permute-start.4
  668.2 0.1 iota_compare_fusion
  668.3 5.8 collective-permute-done.4
  674.1 0.8 fusion.5
  (14 shorter events, 0.1 us)
Async XLA Ops:
  6.5 112.7 %all-gather.3.cloned.1.call-start = ((), (), s32[]{:S(2)}) async-start(), calls=%async_computation.4 | async-start | bytes 5242880 | tf_op jit(solution)/shard_map/all_gather | solution.py:29
  62.1 177.9 %all-gather.5.cloned.1.call-start = ((), (), s32[]{:S(2)}) async-start(), calls=%async_computation.5 | async-start | bytes 5898240 | tf_op jit(solution)/shard_map/all_gather | solution.py:31
  108.4 400.9 %reduce-scatter.3.cloned.1.call-start = ((), (), s32[]{:S(2)}) async-start(), calls=%async_computation.6 | async-start | bytes 11141120 | tf_op jit(solution)/shard_map/reduce_scatter | solution.py:39
  264.1 247.4 %copy-start.2 = (s32[1,5]{1,0:T(1,128)S(1)}, s32[1,5]{1,0:T(1,128)}, u32[]{:S(2)}) copy-start(s32[1,5]{1,0:T(1,128)} %param.5) | copy-start | bytes 64
  264.2 410.0 %copy-start.1 = (f32[1,5,16,256]{3,2,1,0:T(8,128)S(1)}, f32[1,5,16,256]{3,2,1,0:T(8,128)}, u32[]{:S(2)}) copy-start(f32[1,5,16,256]{3,2,1,0:T(8,128)} %param.4) | copy-start | bytes 245764
  264.2 306.2 %reduce-scatter.5.cloned.1.call-start = ((), (), s32[]{:S(2)}) async-start(), calls=%async_computation.7 | async-start | bytes 737280 | tf_op jit(solution)/shard_map/reduce_scatter | solution.py:40
  570.4 103.7 %copy-start = (f32[1,5,16,256]{3,2,1,0:T(8,128)S(1)}, f32[1,5,16,256]{3,2,1,0:T(8,128)}, u32[]{:S(2)}) copy-start(f32[1,5,16,256]{3,2,1,0:T(8,128)} %reduce-scatter.5.cloned.1.call-done) | copy-start | bytes 245764
  585.0 29.2 %all-to-all-start.1 = ((f32[16,1,1280]{2,1,0:T(1,128)}), f32[16,1,1280]{2,1,0:T(1,128)S(1)}, u32[]{:S(2)}, u32[]{:S(2)}) async-start(f32[16,1,1280]{2,1,0:T(1,128)} %reshape.320), calls=%async_computation.3 | async-start | bytes 163840 | tf_op jit(solution)/shard_map/all_to_all | solution.py:42
  616.9 15.0 %collective-permute-start = (f32[5,16,256]{2,1,0:T(8,128)S(1)}, f32[5,16,256]{2,1,0:T(8,128)S(1)}, u32[]{:S(2)}, u32[]{:S(2)}) collective-permute-start(f32[5,16,256]{2,1,0:T(8,128)S(1)} %gather_fusion.1), channel_id=1, source_target_pairs={{16,0},{32,16},{48,32},{64,48},{80,64},{96,80},{112,96},{128,112},... | collective-permute-start | bytes 245768 | tf_op jit(solution)/shard_map/ppermute | solution.py:51
  632.0 14.2 %collective-permute-start.1 = (f32[5,16,256]{2,1,0:T(8,128)S(1)}, f32[5,16,256]{2,1,0:T(8,128)S(1)}, u32[]{:S(2)}, u32[]{:S(2)}) collective-permute-start(f32[5,16,256]{2,1,0:T(8,128)S(1)} %broadcast_select_fusion), channel_id=1, source_target_pairs={{32,0},{48,16},{64,32},{80,48},{96,64},{112,80},{128,96},{144,112}... | collective-permute-start | bytes 245768 | tf_op jit(solution)/shard_map/ppermute | solution.py:51
  646.3 12.3 %collective-permute-start.2 = (f32[5,16,256]{2,1,0:T(8,128)S(1)}, f32[5,16,256]{2,1,0:T(8,128)S(1)}, u32[]{:S(2)}, u32[]{:S(2)}) collective-permute-start(f32[5,16,256]{2,1,0:T(8,128)S(1)} %broadcast_select_fusion.1), channel_id=1, source_target_pairs={{64,0},{80,16},{96,32},{112,48},{128,64},{144,80},{160,96},{176,11... | collective-permute-start | bytes 245768 | tf_op jit(solution)/shard_map/ppermute | solution.py:51
  658.7 7.5 %collective-permute-start.3 = (f32[5,16,256]{2,1,0:T(8,128)S(1)}, f32[5,16,256]{2,1,0:T(8,128)S(1)}, u32[]{:S(2)}, u32[]{:S(2)}) collective-permute-start(f32[5,16,256]{2,1,0:T(8,128)S(1)} %broadcast_select_fusion.2), channel_id=1, source_target_pairs={{128,0},{144,16},{160,32},{176,48},{192,64},{208,80},{224,96},{240... | collective-permute-start | bytes 245768 | tf_op jit(solution)/shard_map/ppermute | solution.py:51
  666.3 7.8 %collective-permute-start.4 = (f32[5,16,256]{2,1,0:T(8,128)S(1)}, f32[5,16,256]{2,1,0:T(8,128)S(1)}, u32[]{:S(2)}, u32[]{:S(2)}) collective-permute-start(f32[5,16,256]{2,1,0:T(8,128)S(1)} %broadcast_select_fusion.3), channel_id=1, source_target_pairs={{256,0},{272,16},{288,32},{304,48},{320,64},{336,80},{352,96},{368... | collective-permute-start | bytes 245768 | tf_op jit(solution)/shard_map/ppermute | solution.py:51
Sparse Core Ops, SparseCore 0:
  62.2 56.9 all-gather.2
  121.4 118.6 all-gather.4
  264.3 245.0 reduce-scatter.2
  512.3 58.1 reduce-scatter.4
